TPU v7x, 32 devices: a whole 2x2x4 slice. The times are simulated.
32 devices in a mesh: party: 2 (over x), dp: 16 (over z, y, core).
Axes of the slice: x: 2, y: 2, z: 4, core: 2. Of those that a mesh axis runs over, the one named last changes fastest.
Arguments:
- x_share: float32 [2, 8192, 1024], P('party', 'dp'), may hold values from -6 to 6
- w_share: float32 [2, 1024, 2048], P('party', 'dp'), may hold values from -0.1875 to 0.1875
- g_share: float32 [2, 8192, 2048], P('party', 'dp'), may hold values from -0.0625 to 0.0625
- fwd_a: float32 [2, 8192, 1024], P('party', 'dp'), may hold values from -4 to 4
- fwd_b: float32 [2, 1024, 2048], P('party', 'dp'), may hold values from -0.125 to 0.125
- fwd_c: float32 [2, 8192, 2048], P('party', 'dp'), may hold values from -2100 to 2100, as said below
- bwd_a: float32 [2, 8192, 1024], P('party', 'dp'), may hold values from -4 to 4
- bwd_b: float32 [2, 8192, 2048], P('party', 'dp'), may hold values from -0.044194174 to 0.044194174
- bwd_c: float32 [2, 1024, 2048], P('party', 'dp'), may hold values from -2100 to 2100, as said below
Outputs:
- y_share: float32 [2, 8192, 2048], P('party', 'dp')
- dw_share: float32 [2, 1024, 2048], P('party', 'dp')
Inputs may be any that keep to these rules, and one draw needn't show every extreme that they name: fwd_c[0] + fwd_c[1] equals (fwd_a[0] + fwd_a[1]) (fwd_b[0] + fwd_b[1]) up to float32 rounding. bwd_c[0] + bwd_c[1] equals (bwd_a[0] + bwd_a[1])^T (bwd_b[0] + bwd_b[1]) up to float32 rounding.
All inputs are finite; a program needn't handle non-finite values.
Results may differ from a plain program's by a relative error of at most 0.0001.
Values sent between devices are 32-bit elements; how exact they have to be, the bound alone decides.
A program may use at most 128 MiB of HBM per device.

v0:
```python
import functools

import jax
import jax.numpy as jnp
from jax import lax
from jax.experimental import pallas as pl
from jax.experimental.pallas import tpu as pltpu
from jax.sharding import PartitionSpec as P

MESH = pl.DeviceIdType.MESH
BF16, F32 = jnp.bfloat16, jnp.float32
SUBS = 2
LAG = 2
TILE = 256
WIDE = 512


def position(chip, nc):
    z, y = chip // 2, lax.rem(chip, 2)
    return z + y * (nc - 1 - 2 * z)


def chip_at(spot, nc):
    spot = lax.rem(spot + 2 * nc, nc)
    y = spot // (nc // 2)
    z = spot + y * (nc - 1 - 2 * spot)
    return 2 * z + y


def split(value):
    high = value.astype(BF16)
    return high, (value - high.astype(F32)).astype(BF16)


def product(left, right):
    def dot(a, b):
        return jnp.dot(a, b, preferred_element_type=F32)

    return dot(left[0], right[0]) + (dot(left[1], right[0]) + dot(left[0], right[1]))


def kernel(
    n,
    x_ref,
    g_ref,
    fa_ref,
    fc_ref,
    ba_ref,
    bb_ref,
    w_ref,
    fb_ref,
    bc_ref,
    y_ref,
    dw_ref,
    wts,
    rx,
    ra,
    rg,
    uo,
    ru,
    acc,
    mate,
    slots,
    lefts,
    right,
    sx,
    sx2,
    sa,
    sa2,
    sg,
    sb,
    sg2,
    tiles,
    ybuf,
    own_w,
    got_w,
    delta,
    give,
    got,
    ld_sem,
    tile_sem,
    y_sem,
    lc_sem,
    xs_send,
    xs_recv,
    sw_send,
    sw_recv,
    ag_send,
    ag_recv,
    ac_send,
    ac_recv,
    rs_send,
    rs_recv,
    mt_send,
    mt_recv,
):
    nc = n // 2
    steps = nc - 1
    party, me = lax.axis_index("party"), lax.axis_index("dp")
    core, chip = lax.rem(me, 2), me // 2
    spot = position(chip, nc)
    rows, ff = fb_ref.shape
    tokens, d = x_ref.shape
    quarter, eighth = tokens // 4, tokens // 8
    piece = ff // (2 * SUBS)
    first = party == 0
    other = {"party": 1 - party}
    buddy = {"dp": me + 1 - 2 * core}
    ahead = {"dp": 2 * chip_at(spot + 1, nc) + core}
    behind = {"dp": 2 * chip_at(spot - 1, nc) + core}

    def cols_of(way, sub):
        return pl.ds((way * SUBS + sub) * piece, piece)

    def half_of(way):
        return pl.ds(way * (ff // 2), ff // 2)

    def remote(src, dst, send, recv, device):
        return pltpu.make_async_remote_copy(
            src_ref=src, dst_ref=dst, send_sem=send, recv_sem=recv, device_id=device, device_id_type=MESH
        )

    own_w[...] = w_ref[...] - fb_ref[...]
    barrier = pltpu.get_barrier_semaphore()
    for device in (other, buddy, ahead, behind):
        pl.semaphore_signal(barrier, inc=1, device_id=device, device_id_type=MESH)
    pl.semaphore_wait(barrier, 4)

    def chunk_copies(side, j):
        start = j * 2 * quarter
        k = 1 + 2 * j
        if side == 0:
            everything = pl.ds(start, 2 * quarter)
            tail = pl.ds(start + 3 * eighth, eighth)
            return [
                remote(x_ref.at[everything], rx.at[everything], xs_send.at[k], xs_recv.at[k], other),
                remote(g_ref.at[tail], rg.at[pl.ds(j * eighth, eighth)], xs_send.at[k + 1], xs_recv.at[k + 1], other),
            ]
        head = pl.ds(start, 3 * eighth)
        return [
            remote(x_ref.at[head], rx.at[head], xs_send.at[k], xs_recv.at[k], other),
            remote(ba_ref.at[head], ra.at[head], xs_send.at[k + 1], xs_recv.at[k + 1], other),
        ]

    def mask_copy():
        return remote(own_w, got_w, xs_send.at[0], xs_recv.at[0], other)

    def open_copy():
        return remote(uo, ru, xs_send.at[5], xs_recv.at[5], other)

    def gather_copy(m, way, sub, step):
        owner = chip_at(spot - step, nc) if way == 0 else chip_at(spot + step, nc)
        return remote(
            wts.at[m, owner, core, :, cols_of(way, sub)],
            wts.at[m, owner, core, :, cols_of(way, sub)],
            ag_send.at[m, way, sub, step],
            ag_recv.at[m, way, sub, step],
            ahead if way == 0 else behind,
        )

    def gather_first(m, way, sub, source):
        return remote(
            source.at[:, cols_of(way, sub)],
            wts.at[m, chip, core, :, cols_of(way, sub)],
            ag_send.at[m, way, sub, 0],
            ag_recv.at[m, way, sub, 0],
            ahead if way == 0 else behind,
        )

    def gather_arrival(m, way, sub, step):
        owner = chip_at(spot - 1 - step, nc) if way == 0 else chip_at(spot + 1 + step, nc)
        here = wts.at[m, owner, core, :, cols_of(way, sub)]
        return remote(here, here, ag_send.at[m, way, sub, step], ag_recv.at[m, way, sub, step], ahead)

    def begin_gather(m, source):
        for sub in range(SUBS):
            for way in range(2):
                gather_first(m, way, sub, source).start()
        remote(source, wts.at[m, chip, core], ac_send.at[m], ac_recv.at[m], buddy).start()
        pltpu.make_async_copy(source, wts.at[m, chip, core], lc_sem.at[m]).start()

    def pass_on(m, step):
        for sub in range(SUBS):
            for way in range(2):
                gather_arrival(m, way, sub, step).wait_recv()

                @pl.when(step < steps - 1)
                def _():
                    gather_copy(m, way, sub, step + 1).start()

        for way in range(2):
            owner = chip_at(spot - 1 - step, nc) if way == 0 else chip_at(spot + 1 + step, nc)
            here = wts.at[m, owner, core, :, half_of(way)]
            remote(here, here, ac_send.at[m], ac_recv.at[m], buddy).start()

    def load(src, dst, k):
        return pltpu.make_async_copy(src, dst, ld_sem.at[k])

    def open_rows(i):
        part = pl.ds(pl.multiple_of(i * quarter, 8), quarter)
        copies = [load(x_ref.at[part], sx, 0), load(fa_ref.at[part], sa, 1)]
        for copy in copies:
            copy.start()
        for copy in copies:
            copy.wait()
        sx2[...] = sx[...] - sa[...]
        out = load(sx2, uo.at[part], 2)
        out.start()
        out.wait()

    def put_left(k, at, value):
        high, low = split(value)
        lefts[k, 0, :, at] = high.T
        lefts[k, 1, :, at] = low.T

    def put_right(k, at, value):
        high, low = split(value)
        for half in range(2):
            to = slice(half * 2 * quarter + at.start, half * 2 * quarter + at.stop)
            right[2 * k, to, :] = high[:, half * (ff // 2) : (half + 1) * (ff // 2)]
            right[2 * k + 1, to, :] = low[:, half * (ff // 2) : (half + 1) * (ff // 2)]

    def operands(j):
        for part in range(2):
            start = (2 * j + part) * quarter
            here = pl.ds(start, quarter)
            to = slice(part * quarter, (part + 1) * quarter)
            own = [
                load(x_ref.at[here], sx, 0),
                load(ba_ref.at[here], sa, 1),
                load(g_ref.at[here], sg, 2),
                load(bb_ref.at[here], sb, 3),
            ]
            for copy in own:
                copy.start()

            @pl.when(first)
            def _():
                if part == 0:
                    for copy in chunk_copies(1, j):
                        copy.wait_recv()
                many = quarter if part == 0 else eighth
                some = pl.ds(start, many)
                more = [load(rx.at[some], sx2.at[pl.ds(0, many)], 4), load(ra.at[some], sa2.at[pl.ds(0, many)], 5)]
                for copy in more:
                    copy.start()
                for copy in own + more:
                    copy.wait()
                if part == 1:
                    sx2[many:, :] = jnp.zeros((quarter - many, d), F32)
                    sa2[many:, :] = jnp.zeros((quarter - many, d), F32)
                    sx[many:, :] = jnp.zeros((quarter - many, d), F32)
                    sg[many:, :] = jnp.zeros((quarter - many, ff), F32)
                put_left(0, to, sa2[...])
                put_left(1, to, (sx[...] + sx2[...]) - sa2[...])
                put_left(2, to, sa[...])
                put_right(0, to, sg[...])
                put_right(1, to, sb[...])

            @pl.when(jnp.logical_not(first))
            def _():
                if part == 0:
                    for copy in chunk_copies(0, j):
                        copy.wait_recv()
                more = [load(rx.at[here], sx2, 4)]
                if part == 1:
                    more.append(load(rg.at[pl.ds(j * eighth, eighth)], sg2, 5))
                for copy in more:
                    copy.start()
                for copy in own + more:
                    copy.wait()
                sg[...] = sg[...] - sb[...]
                if part == 1:
                    sg[eighth:, :] = sg[eighth:, :] + sg2[...]
                opened = sx[...] + sx2[...]
                put_left(0, to, opened - sa[...])
                put_left(1, to, sa[...])
                put_left(2, to, opened)
                put_right(0, to, sg[...])
                put_right(1, to, sb[...])

    keep = jnp.where(first, 1.0, 0.0).astype(F32)
    sign = 1.0 - 2.0 * keep
    group = d // 4
    per = group // (2 * rows)

    def gradient_rows(j, q):
        at = pl.ds(pl.multiple_of(q * group, group), group)
        chips = pl.ds(q * per, per)

        def tile(t, carry):
            half = t // (ff // 2 // WIDE)
            deep = pl.ds(pl.multiple_of(half * 2 * quarter, 2 * quarter), 2 * quarter)
            wide = pl.ds(pl.multiple_of(lax.rem(t, ff // 2 // WIDE) * WIDE, WIDE), WIDE)
            cols = pl.ds(pl.multiple_of(t * WIDE, WIDE), WIDE)

            def multiply(k, m):
                return product(
                    (lefts[k, 0, at, :], lefts[k, 1, at, :]),
                    (right[2 * m, deep, wide], right[2 * m + 1, deep, wide]),
                )

            shared = multiply(2, 1)
            shape = (per, 2, rows, WIDE)
            foreign = (multiply(0, 0) + keep * shared).reshape(shape)
            mine = (multiply(1, 0) + sign * shared).reshape(shape)
            if j == 0:
                acc[0, chips, :, :, cols] = foreign
                acc[1, chips, :, :, cols] = mine
            else:
                acc[0, chips, :, :, cols] = acc[0, chips, :, :, cols] + foreign
                acc[1, chips, :, :, cols] = acc[1, chips, :, :, cols] + mine
            return carry

        lax.fori_loop(0, ff // WIDE, tile, 0)

    begin_gather(0, fb_ref)
    mask_copy().start()
    for side in range(2):

        @pl.when(party == side)
        def _():
            for j in range(2):
                for copy in chunk_copies(side, j):
                    copy.start()

    early = steps - 3

    def gather_step(i, carry):
        @pl.when(i < steps)
        def _():
            pass_on(0, i)

        @pl.when(i < 4)
        def _():
            open_rows(i)

        @pl.when(i == 3)
        def _():
            open_copy().start()

        @pl.when(i == early)
        def _():
            operands(0)

        @pl.when(i > early)
        def _():
            @pl.when(i <= early + 2)
            def _():
                gradient_rows(0, 2 * (i - early - 1))

        @pl.when(i == LAG - 1)
        def _():
            mask_copy().wait_recv()
            delta[...] = own_w[...] + got_w[...]
            begin_gather(1, delta)

        @pl.when(i >= LAG)
        def _():
            pass_on(1, i - LAG)

        @pl.when(i > early)
        def _():
            @pl.when(i <= early + 2)
            def _():
                gradient_rows(0, 2 * (i - early - 1) + 1)

        return carry

    lax.fori_loop(0, steps + LAG, gather_step, 0)

    operands(1)

    def second(q, carry):
        gradient_rows(1, q)
        return carry

    lax.fori_loop(0, 4, second, 0)

    def mate_copy(m, to_chip):
        return remote(acc.at[m, to_chip, 1 - core], mate.at[m, to_chip], mt_send.at[m], mt_recv.at[m, to_chip], buddy)

    def mate_pair(k, carry):
        for m in range(2):
            mate_copy(m, chip_at(spot - k, nc)).start()
            mate_copy(m, chip_at(spot + k, nc)).start()
        return carry

    lax.fori_loop(1, nc // 2, mate_pair, 0)
    for m in range(2):
        mate_copy(m, chip_at(spot + nc // 2, nc)).start()
    for m in range(2):
        mate_copy(m, chip).start()
    fetch_y = load(fc_ref, ybuf, 6)
    fetch_y.start()
    for m in range(2):
        pltpu.make_async_copy(wts.at[m, chip, core], wts.at[m, chip, core], lc_sem.at[m]).wait()
        everything = remote(wts.at[m, :, core], wts.at[m, :, 1 - core], ac_send.at[m], ac_recv.at[m], buddy)
        everything.wait_recv()
        everything.wait_send()

    def owner_of(way, step):
        return chip_at(spot - 1 - step, nc) if way == 0 else chip_at(spot + 1 + step, nc)

    def sum_copy(m, way, sub, step, source):
        return remote(
            source,
            slots.at[m, way, sub, step],
            rs_send.at[m, way, sub, step],
            rs_recv.at[m, way, sub, step],
            ahead if way == 0 else behind,
        )

    def mate_arrivals(m, step):
        mate_copy(m, owner_of(0, step)).wait_recv()

        @pl.when(step < nc // 2 - 1)
        def _():
            mate_copy(m, owner_of(1, step)).wait_recv()

    def sum_start(m):
        mate_arrivals(m, 0)
        for sub in range(SUBS):
            for way in range(2):
                owner, cols = owner_of(way, 0), cols_of(way, sub)
                acc[m, owner, core, :, cols] = acc[m, owner, core, :, cols] + mate[m, owner, :, cols]
                sum_copy(m, way, sub, 0, acc.at[m, owner, core, :, cols]).start()

    def sum_step(m, step):
        @pl.when(step < nc // 2)
        def _():
            mate_arrivals(m, step)

        for sub in range(SUBS):
            for way in range(2):
                owner, cols = owner_of(way, step), cols_of(way, sub)
                held = slots.at[m, way, sub, step - 1]
                sum_copy(m, way, sub, step - 1, held).wait_recv()
                slots[m, way, sub, step - 1] = slots[m, way, sub, step - 1] + (
                    acc[m, owner, core, :, cols] + mate[m, owner, :, cols]
                )
                sum_copy(m, way, sub, step, held).start()

    nt = ff // TILE

    def fetch(m, t, buf):
        cols = pl.ds(pl.multiple_of(t * TILE, TILE), TILE)
        return pltpu.make_async_copy(wts.at[m, :, :, :, cols], tiles.at[m, buf], tile_sem.at[m, buf])

    def put_rows(k, i, value):
        high, low = split(value)
        to = pl.ds(pl.multiple_of(i * quarter, quarter), quarter)
        right[k, to, :] = high
        right[k + 1, to, :] = low

    def factor_rows(i, carry):
        here = pl.ds(pl.multiple_of(i * quarter, quarter), quarter)
        copy = load(fa_ref.at[here], sa, 0)
        copy.start()
        copy.wait()
        put_rows(0, i, sa[...])
        return carry

    def opened_rows(i, carry):
        here = pl.ds(pl.multiple_of(i * quarter, quarter), quarter)
        copies = [load(uo.at[here], sx, 0), load(ru.at[here], sx2, 1)]
        for copy in copies:
            copy.start()
        for copy in copies:
            copy.wait()
        put_rows(2, i, sx[...] + sx2[...])
        return carry

    def first_tile(t):
        buf = lax.rem(t, 2)
        cols = pl.ds(pl.multiple_of(t * TILE, TILE), TILE)

        @pl.when(t + 1 < nt)
        def _():
            fetch(1, t + 1, lax.rem(t + 1, 2)).start()

        fetch(1, t, buf).wait()
        weight = split(tiles[1, buf].reshape(d, TILE))
        ybuf[:, cols] = ybuf[:, cols] + product((right[0], right[1]), weight)

    def second_tile(t):
        buf = lax.rem(t, 2)
        cols = pl.ds(pl.multiple_of(t * TILE, TILE), TILE)

        @pl.when(t + 1 < nt)
        def _():
            for m in range(2):
                fetch(m, t + 1, lax.rem(t + 1, 2)).start()

        for m in range(2):
            fetch(m, t, buf).wait()
        weight = split(tiles[0, buf].reshape(d, TILE) + keep * tiles[1, buf].reshape(d, TILE))
        ybuf[:, cols] = ybuf[:, cols] + product((right[2], right[3]), weight)
        pltpu.make_async_copy(ybuf.at[:, cols], y_ref.at[:, cols], y_sem.at[t]).start()

    for m in range(2):
        sum_start(m)

    def forward(work):
        @pl.when(work == 0)
        def _():
            fetch(1, 0, 0).start()
            lax.fori_loop(0, 4, factor_rows, 0)
            fetch_y.wait()

        @pl.when(work < nt // 2)
        def _():
            first_tile(2 * work)
            first_tile(2 * work + 1)

        @pl.when(work == late)
        def _():
            for m in range(2):
                fetch(m, 0, 0).start()
            open_copy().wait_recv()
            lax.fori_loop(0, 4, opened_rows, 0)

        @pl.when(jnp.logical_and(work >= late, work < late + nt // 2))
        def _():
            second_tile(2 * (work - late))
            second_tile(2 * (work - late) + 1)

    late = 2 * (steps - 1) - nt // 2 - 1

    def ring_step(step, carry):
        forward(2 * (step - 1))
        sum_step(0, step)
        forward(2 * (step - 1) + 1)
        sum_step(1, step)
        return carry

    lax.fori_loop(1, steps, ring_step, 0)

    def swap_copy(way, sub):
        cols = cols_of(way, sub)
        return remote(give.at[:, cols], got.at[:, cols], sw_send.at[way, sub], sw_recv.at[way, sub], other)

    def total(m, way, sub):
        cols = cols_of(way, sub)
        held = slots.at[m, way, sub, steps - 1]
        sum_copy(m, way, sub, steps - 1, held).wait_recv()
        return slots[m, way, sub, steps - 1] + (acc[m, chip, core, :, cols] + mate[m, chip, :, cols])

    for m in range(2):
        mate_copy(m, chip).wait_recv()
    for sub in range(SUBS):
        for way in range(2):
            cols = cols_of(way, sub)
            give[:, cols] = total(0, way, sub) - keep * bc_ref[:, cols]
            swap_copy(way, sub).start()
    for sub in range(SUBS):
        for way in range(2):
            cols = cols_of(way, sub)
            dw_ref[:, cols] = total(1, way, sub) + keep * bc_ref[:, cols]
    for sub in range(SUBS):
        for way in range(2):
            cols = cols_of(way, sub)
            swap_copy(way, sub).wait_recv()
            dw_ref[:, cols] = dw_ref[:, cols] + got[:, cols]

    def drain(step, carry):
        for m in range(2):
            for way in range(2):
                for sub in range(SUBS):
                    gather_copy(m, way, sub, step).wait_send()
                    sum_copy(m, way, sub, step, slots.at[m, way, sub, step]).wait_send()
        return carry

    lax.fori_loop(0, steps, drain, 0)
    for m in range(2):
        remote(acc.at[m, :, 1 - core], mate.at[m], mt_send.at[m], mt_recv.at[m, 0], buddy).wait_send()
    mask_copy().wait_send()
    open_copy().wait_send()
    for side in range(2):

        @pl.when(party == side)
        def _():
            for j in range(2):
                for copy in chunk_copies(side, j):
                    copy.wait_send()

    for way in range(2):
        for sub in range(SUBS):
            swap_copy(way, sub).wait_send()
    for t in range(nt):
        cols = pl.ds(t * TILE, TILE)
        pltpu.make_async_copy(ybuf.at[:, cols], y_ref.at[:, cols], y_sem.at[t]).wait()


def body(n, x_share, w_share, g_share, fwd_a, fwd_b, fwd_c, bwd_a, bwd_b, bwd_c):
    tokens, d = x_share.shape[1:]
    rows, ff = fwd_b.shape[1:]
    nc = n // 2
    steps = nc - 1
    quarter, eighth = tokens // 4, tokens // 8
    piece = ff // (2 * SUBS)
    hbm = pl.BlockSpec(memory_space=pl.ANY)
    vmem = pl.BlockSpec(memory_space=pltpu.VMEM)
    dma = pltpu.SemaphoreType.DMA

    def shape(*dims):
        return jax.ShapeDtypeStruct(dims, F32)

    outs = pl.pallas_call(
        functools.partial(kernel, n),
        out_shape=[
            shape(tokens, ff),
            shape(rows, ff),
            shape(2, nc, 2, rows, ff),
            shape(tokens, d),
            shape(tokens, d),
            shape(tokens // 4, ff),
            shape(tokens, d),
            shape(tokens, d),
        ],
        in_specs=[hbm] * 6 + [vmem] * 3,
        out_specs=[hbm, vmem] + [hbm] * 6,
        scratch_shapes=[
            pltpu.VMEM((2, nc, 2, rows, ff), F32),
            pltpu.VMEM((2, nc, rows, ff), F32),
            pltpu.VMEM((2, 2, SUBS, steps, rows, piece), F32),
            pltpu.VMEM((3, 2, d, 2 * quarter), BF16),
            pltpu.VMEM((4, 4 * quarter, ff // 2), BF16),
            pltpu.VMEM((quarter, d), F32),
            pltpu.VMEM((quarter, d), F32),
            pltpu.VMEM((quarter, d), F32),
            pltpu.VMEM((quarter, d), F32),
            pltpu.VMEM((quarter, ff), F32),
            pltpu.VMEM((quarter, ff), F32),
            pltpu.VMEM((eighth, ff), F32),
            pltpu.VMEM((2, 2, nc, 2, rows, TILE), F32),
            pltpu.VMEM((tokens, ff), F32),
            pltpu.VMEM((rows, ff), F32),
            pltpu.VMEM((rows, ff), F32),
            pltpu.VMEM((rows, ff), F32),
            pltpu.VMEM((rows, ff), F32),
            pltpu.VMEM((rows, ff), F32),
            dma((7,)),
            dma((2, 2)),
            dma((ff // TILE,)),
            dma((2,)),
            dma((6,)),
            dma((6,)),
            dma((2, SUBS)),
            dma((2, SUBS)),
            dma((2, 2, SUBS, steps)),
            dma((2, 2, SUBS, steps)),
            dma((2,)),
            dma((2,)),
            dma((2, 2, SUBS, steps)),
            dma((2, 2, SUBS, steps)),
            dma((2,)),
            dma((2, nc)),
        ],
        compiler_params=pltpu.CompilerParams(collective_id=0, has_side_effects=True, vmem_limit_bytes=66_500_000),
        cost_estimate=pl.CostEstimate(flops=32 * tokens * d * ff, bytes_accessed=100 * 2**20, transcendentals=0),
    )(
        x_share[0],
        g_share[0],
        fwd_a[0],
        fwd_c[0],
        bwd_a[0],
        bwd_b[0],
        w_share[0],
        fwd_b[0],
        bwd_c[0],
    )
    return outs[0][None], outs[1][None]


def solution(mesh):
    spec = P("party", "dp", None)
    return jax.shard_map(
        functools.partial(body, mesh.shape["dp"]),
        mesh=mesh,
        in_specs=(spec,) * 9,
        out_specs=(spec, spec),
        check_vma=False,
    )
```

profile of v0, /device:TPU:0, one launch (start us, length us, event | category | flops | bytes accessed | tf_op | source)
XLA Modules:
  0.0 199.6 jit_solution(15781413092841202217)
XLA Ops:
  0.6 193.4 %shard_map.104 = (f32[512,2048]{1,0:T(8,128)}, f32[64,2048]{1,0:T(8,128)}, f32[2,8,2,64,2048]{4,3,2,1,0:T(8,128)}, f32[512,1024]{1,0:T(8,128)}, f32[512,1024]{1,...) custom-call(f32[512,1024]{1,0:T(8,128)} %bitcast.16, f32[512,2048]{1,0:T(8,128)} %bitcast.13, ...), custom_call_target="tpu_custom_call" | custom-call | flops 34359738368 | bytes 104857600 | tf_op jit(solution)/shard_map/pallas_call | solution.py:609
  194.0 0.0 copy-start
  194.0 4.8 %copy.13 = f32[1,512,2048]{2,1,0:T(8,128)} copy(f32[1,512,2048]{2,1,0:T(8,128)} %bitcast.11) | data formatting | bytes 8388608
  198.8 0.0 copy-done
  198.8 0.8 copy.14
Async XLA Ops:
  194.0 4.8 %copy-start = (f32[64,2048]{1,0:T(8,128)S(1)}, f32[64,2048]{1,0:T(8,128)}, u32[]{:S(2)}) copy-start(f32[64,2048]{1,0:T(8,128)} %get-tuple-element.5) | copy-start | bytes 1572868
where the time goes:
time: 203 us; the launch traced here: 200 us
  Pallas kernels  193 us (95%)
  local copies, waits for them, and re-layouts  5.55 us (3%)
    pallas_call x1, Pallas kernels, body(): pl.pallas_call(functools.partial(kernel, n), out_shape=[shape(tokens, ff)...  193 us
    unnamed x4, local copies, waits for them, and re-layouts  5.55 us

commit v1 on v0

--- a/solution.py
+++ b/solution.py
@@ -12,7 +12,7 @@
 SUBS = 2
 LAG = 2
 TILE = 256
-WIDE = 512
+WIDE = 1024
 
 
 def position(chip, nc):
@@ -198,13 +198,14 @@
 
     def open_rows(i):
         part = pl.ds(pl.multiple_of(i * quarter, 8), quarter)
-        copies = [load(x_ref.at[part], sx, 0), load(fa_ref.at[part], sa, 1)]
+        at = pl.ds(0, quarter)
+        copies = [load(x_ref.at[part], sx.at[at], 0), load(fa_ref.at[part], sa.at[at], 1)]
         for copy in copies:
             copy.start()
         for copy in copies:
             copy.wait()
-        sx2[...] = sx[...] - sa[...]
-        out = load(sx2, uo.at[part], 2)
+        sx2[:quarter, :] = sx[:quarter, :] - sa[:quarter, :]
+        out = load(sx2.at[at], uo.at[part], 2)
         out.start()
         out.wait()
 
@@ -220,71 +221,89 @@
             right[2 * k, to, :] = high[:, half * (ff // 2) : (half + 1) * (ff // 2)]
             right[2 * k + 1, to, :] = low[:, half * (ff // 2) : (half + 1) * (ff // 2)]
 
-    def operands(j):
+    def owned(j):
+        start = 2 * j * quarter
+        both = pl.ds(start, 2 * quarter)
+        rest = [load(x_ref.at[both], sx, 0), load(ba_ref.at[both], sa, 1)]
+        for copy in rest:
+            copy.start()
         for part in range(2):
-            start = (2 * j + part) * quarter
-            here = pl.ds(start, quarter)
+            here = pl.ds(start + part * quarter, quarter)
             to = slice(part * quarter, (part + 1) * quarter)
-            own = [
-                load(x_ref.at[here], sx, 0),
-                load(ba_ref.at[here], sa, 1),
-                load(g_ref.at[here], sg, 2),
-                load(bb_ref.at[here], sb, 3),
-            ]
+            own = [load(g_ref.at[here], sg, 2), load(bb_ref.at[here], sb, 3)]
             for copy in own:
                 copy.start()
+            for copy in own:
+                copy.wait()
+            put_right(1, to, sb[...])
 
             @pl.when(first)
             def _():
-                if part == 0:
-                    for copy in chunk_copies(1, j):
-                        copy.wait_recv()
-                many = quarter if part == 0 else eighth
-                some = pl.ds(start, many)
-                more = [load(rx.at[some], sx2.at[pl.ds(0, many)], 4), load(ra.at[some], sa2.at[pl.ds(0, many)], 5)]
-                for copy in more:
-                    copy.start()
-                for copy in own + more:
-                    copy.wait()
                 if part == 1:
-                    sx2[many:, :] = jnp.zeros((quarter - many, d), F32)
-                    sa2[many:, :] = jnp.zeros((quarter - many, d), F32)
-                    sx[many:, :] = jnp.zeros((quarter - many, d), F32)
-                    sg[many:, :] = jnp.zeros((quarter - many, ff), F32)
-                put_left(0, to, sa2[...])
-                put_left(1, to, (sx[...] + sx2[...]) - sa2[...])
-                put_left(2, to, sa[...])
+                    sg[eighth:, :] = jnp.zeros((eighth, ff), F32)
                 put_right(0, to, sg[...])
-                put_right(1, to, sb[...])
 
             @pl.when(jnp.logical_not(first))
             def _():
-                if part == 0:
-                    for copy in chunk_copies(0, j):
-                        copy.wait_recv()
-                more = [load(rx.at[here], sx2, 4)]
-                if part == 1:
-                    more.append(load(rg.at[pl.ds(j * eighth, eighth)], sg2, 5))
-                for copy in more:
-                    copy.start()
-                for copy in own + more:
-                    copy.wait()
                 sg[...] = sg[...] - sb[...]
-                if part == 1:
-                    sg[eighth:, :] = sg[eighth:, :] + sg2[...]
-                opened = sx[...] + sx2[...]
-                put_left(0, to, opened - sa[...])
-                put_left(1, to, sa[...])
-                put_left(2, to, opened)
                 put_right(0, to, sg[...])
-                put_right(1, to, sb[...])
+
+        for copy in rest:
+            copy.wait()
+        whole = slice(0, 2 * quarter)
+
+        @pl.when(first)
+        def _():
+            put_left(2, whole, sa[...])
+
+        @pl.when(jnp.logical_not(first))
+        def _():
+            put_left(1, whole, sa[...])
+
+    def received(j):
+        start = 2 * j * quarter
+        whole = slice(0, 2 * quarter)
+        many = 3 * eighth
+
+        @pl.when(first)
+        def _():
+            for copy in chunk_copies(1, j):
+                copy.wait_recv()
+            some = pl.ds(start, many)
+            more = [load(rx.at[some], sx2.at[pl.ds(0, many)], 4), load(ra.at[some], sa2.at[pl.ds(0, many)], 5)]
+            for copy in more:
+                copy.start()
+            for copy in more:
+                copy.wait()
+            sx2[many:, :] = jnp.zeros((eighth, d), F32)
+            sa2[many:, :] = jnp.zeros((eighth, d), F32)
+            sx[many:, :] = jnp.zeros((eighth, d), F32)
+            put_left(0, whole, sa2[...])
+            put_left(1, whole, (sx[...] + sx2[...]) - sa2[...])
+
+        @pl.when(jnp.logical_not(first))
+        def _():
+            for copy in chunk_copies(0, j):
+                copy.wait_recv()
+            more = [
+                load(rx.at[pl.ds(start, 2 * quarter)], sx2, 4),
+                load(rg.at[pl.ds(j * eighth, eighth)], sg2, 5),
+            ]
+            for copy in more:
+                copy.start()
+            for copy in more:
+                copy.wait()
+            put_right(0, slice(many, 2 * quarter), sg[eighth:, :] + sg2[...])
+            sx[...] = sx[...] + sx2[...]
+            put_left(0, whole, sx[...] - sa[...])
+            put_left(2, whole, sx[...])
 
     keep = jnp.where(first, 1.0, 0.0).astype(F32)
     sign = 1.0 - 2.0 * keep
     group = d // 4
     per = group // (2 * rows)
 
-    def gradient_rows(j, q):
+    def gradient_rows(j, q, tile_from, tile_to):
         at = pl.ds(pl.multiple_of(q * group, group), group)
         chips = pl.ds(q * per, per)
 
@@ -312,7 +331,7 @@
                 acc[1, chips, :, :, cols] = acc[1, chips, :, :, cols] + mine
             return carry
 
-        lax.fori_loop(0, ff // WIDE, tile, 0)
+        lax.fori_loop(tile_from, tile_to, tile, 0)
 
     begin_gather(0, fb_ref)
     mask_copy().start()
@@ -341,13 +360,14 @@
 
         @pl.when(i == early)
         def _():
-            operands(0)
+            owned(0)
+            received(0)
 
         @pl.when(i > early)
         def _():
             @pl.when(i <= early + 2)
             def _():
-                gradient_rows(0, 2 * (i - early - 1))
+                gradient_rows(0, 2 * (i - early - 1), 0, ff // WIDE)
 
         @pl.when(i == LAG - 1)
         def _():
@@ -363,41 +383,46 @@
         def _():
             @pl.when(i <= early + 2)
             def _():
-                gradient_rows(0, 2 * (i - early - 1) + 1)
+                gradient_rows(0, 2 * (i - early - 1) + 1, 0, ff // WIDE)
 
         return carry
 
-    lax.fori_loop(0, steps + LAG, gather_step, 0)
-
-    operands(1)
-
-    def second(q, carry):
-        gradient_rows(1, q)
-        return carry
-
-    lax.fori_loop(0, 4, second, 0)
-
-    def mate_copy(m, to_chip):
-        return remote(acc.at[m, to_chip, 1 - core], mate.at[m, to_chip], mt_send.at[m], mt_recv.at[m, to_chip], buddy)
-
-    def mate_pair(k, carry):
-        for m in range(2):
-            mate_copy(m, chip_at(spot - k, nc)).start()
-            mate_copy(m, chip_at(spot + k, nc)).start()
-        return carry
-
-    lax.fori_loop(1, nc // 2, mate_pair, 0)
-    for m in range(2):
-        mate_copy(m, chip_at(spot + nc // 2, nc)).start()
-    for m in range(2):
-        mate_copy(m, chip).start()
+    lax.fori_loop(0, steps + LAG - 1, gather_step, 0)
+
+    owned(1)
+    received(1)
+    zs, span = nc // 2, nc // 8
+
+    def group_at(way, k):
+        place = jnp.where(way == 0, spot, nc - 1 - spot)
+        falling = (place + span - 1) // span
+        rising = (nc - place) // span
+        low = jnp.where(k < falling, falling - 1 - k, k)
+        high = jnp.where(k < 4 - rising, rising + k, 3 - k)
+        return jnp.where(place <= zs, low, high)
+
+    def mate_copy(m, way, k):
+        chips = pl.ds(group_at(way, k) * per, per)
+        cols = pl.ds(pl.multiple_of(way * (ff // 2), 128), ff // 2)
+        return remote(
+            acc.at[m, chips, 1 - core, :, cols],
+            mate.at[m, chips, :, cols],
+            mt_send.at[m, way, k],
+            mt_recv.at[m, way, k],
+            buddy,
+        )
+
+    def second(k):
+        def one(way, carry):
+            gradient_rows(1, group_at(way, k), way * (ff // 2 // WIDE), (way + 1) * (ff // 2 // WIDE))
+            for m in range(2):
+                mate_copy(m, way, k).start()
+            return carry
+
+        lax.fori_loop(0, 2, one, 0)
+
     fetch_y = load(fc_ref, ybuf, 6)
     fetch_y.start()
-    for m in range(2):
-        pltpu.make_async_copy(wts.at[m, chip, core], wts.at[m, chip, core], lc_sem.at[m]).wait()
-        everything = remote(wts.at[m, :, core], wts.at[m, :, 1 - core], ac_send.at[m], ac_recv.at[m], buddy)
-        everything.wait_recv()
-        everything.wait_send()
 
     def owner_of(way, step):
         return chip_at(spot - 1 - step, nc) if way == 0 else chip_at(spot + 1 + step, nc)
@@ -412,11 +437,8 @@
         )
 
     def mate_arrivals(m, step):
-        mate_copy(m, owner_of(0, step)).wait_recv()
-
-        @pl.when(step < nc // 2 - 1)
-        def _():
-            mate_copy(m, owner_of(1, step)).wait_recv()
+        for way in range(2):
+            mate_copy(m, way, step).wait_recv()
 
     def sum_start(m):
         mate_arrivals(m, 0)
@@ -427,7 +449,7 @@
                 sum_copy(m, way, sub, 0, acc.at[m, owner, core, :, cols]).start()
 
     def sum_step(m, step):
-        @pl.when(step < nc // 2)
+        @pl.when(step < 4)
         def _():
             mate_arrivals(m, step)
 
@@ -449,27 +471,25 @@
 
     def put_rows(k, i, value):
         high, low = split(value)
-        to = pl.ds(pl.multiple_of(i * quarter, quarter), quarter)
+        to = pl.ds(i * 2 * quarter, 2 * quarter)
         right[k, to, :] = high
         right[k + 1, to, :] = low
 
-    def factor_rows(i, carry):
-        here = pl.ds(pl.multiple_of(i * quarter, quarter), quarter)
+    def factor_rows(i):
+        here = pl.ds(i * 2 * quarter, 2 * quarter)
         copy = load(fa_ref.at[here], sa, 0)
         copy.start()
         copy.wait()
         put_rows(0, i, sa[...])
-        return carry
-
-    def opened_rows(i, carry):
-        here = pl.ds(pl.multiple_of(i * quarter, quarter), quarter)
+
+    def opened_rows(i):
+        here = pl.ds(i * 2 * quarter, 2 * quarter)
         copies = [load(uo.at[here], sx, 0), load(ru.at[here], sx2, 1)]
         for copy in copies:
             copy.start()
         for copy in copies:
             copy.wait()
         put_rows(2, i, sx[...] + sx2[...])
-        return carry
 
     def first_tile(t):
         buf = lax.rem(t, 2)
@@ -477,7 +497,7 @@
 
         @pl.when(t + 1 < nt)
         def _():
-            fetch(1, t + 1, lax.rem(t + 1, 2)).start()
+            fetch(1, t + 1, 1 - buf).start()
 
         fetch(1, t, buf).wait()
         weight = split(tiles[1, buf].reshape(d, TILE))
@@ -490,7 +510,7 @@
         @pl.when(t + 1 < nt)
         def _():
             for m in range(2):
-                fetch(m, t + 1, lax.rem(t + 1, 2)).start()
+                fetch(m, t + 1, 1 - buf).start()
 
         for m in range(2):
             fetch(m, t, buf).wait()
@@ -498,43 +518,50 @@
         ybuf[:, cols] = ybuf[:, cols] + product((right[2], right[3]), weight)
         pltpu.make_async_copy(ybuf.at[:, cols], y_ref.at[:, cols], y_sem.at[t]).start()
 
-    for m in range(2):
-        sum_start(m)
+    second(0)
+    sum_start(0)
+    second(1)
+    pass_on(1, steps - 1)
+    late = 2 * steps - 6
+
+    def several(tile, turn):
+        def one(t, carry):
+            tile(t)
+            return carry
+
+        lax.fori_loop(turn * nt // 3, (turn + 1) * nt // 3, one, 0)
 
     def forward(work):
-        @pl.when(work == 0)
-        def _():
+        @pl.when(work == 3)
+        def _():
+            for m in range(2):
+                pltpu.make_async_copy(wts.at[m, chip, core], wts.at[m, chip, core], lc_sem.at[m]).wait()
+                everything = remote(wts.at[m, :, core], wts.at[m, :, 1 - core], ac_send.at[m], ac_recv.at[m], buddy)
+                everything.wait_recv()
+                everything.wait_send()
             fetch(1, 0, 0).start()
-            lax.fori_loop(0, 4, factor_rows, 0)
             fetch_y.wait()
 
-        @pl.when(work < nt // 2)
-        def _():
-            first_tile(2 * work)
-            first_tile(2 * work + 1)
+        @pl.when(work == 4)
+        def _():
+            factor_rows(0)
+            factor_rows(1)
+
+        @pl.when(jnp.logical_and(work >= 5, work < 8))
+        def _():
+            several(first_tile, work - 5)
+
+        @pl.when(jnp.logical_and(work > late, work <= late + 3))
+        def _():
+            several(second_tile, work - late - 1)
 
         @pl.when(work == late)
         def _():
             for m in range(2):
                 fetch(m, 0, 0).start()
             open_copy().wait_recv()
-            lax.fori_loop(0, 4, opened_rows, 0)
-
-        @pl.when(jnp.logical_and(work >= late, work < late + nt // 2))
-        def _():
-            second_tile(2 * (work - late))
-            second_tile(2 * (work - late) + 1)
-
-    late = 2 * (steps - 1) - nt // 2 - 1
-
-    def ring_step(step, carry):
-        forward(2 * (step - 1))
-        sum_step(0, step)
-        forward(2 * (step - 1) + 1)
-        sum_step(1, step)
-        return carry
-
-    lax.fori_loop(1, steps, ring_step, 0)
+            for i in range(2):
+                opened_rows(i)
 
     def swap_copy(way, sub):
         cols = cols_of(way, sub)
@@ -546,13 +573,34 @@
         sum_copy(m, way, sub, steps - 1, held).wait_recv()
         return slots[m, way, sub, steps - 1] + (acc[m, chip, core, :, cols] + mate[m, chip, :, cols])
 
-    for m in range(2):
-        mate_copy(m, chip).wait_recv()
-    for sub in range(SUBS):
-        for way in range(2):
-            cols = cols_of(way, sub)
-            give[:, cols] = total(0, way, sub) - keep * bc_ref[:, cols]
-            swap_copy(way, sub).start()
+    def half_step(work, carry):
+        m = lax.rem(work, 2)
+        step = work // 2 + 1 - m
+        forward(work)
+
+        @pl.when(jnp.logical_and(m == 1, step < 2))
+        def _():
+            second(step + 2)
+
+        @pl.when(step == 0)
+        def _():
+            sum_start(1)
+
+        @pl.when(jnp.logical_and(step > 0, step < steps))
+        def _():
+            sum_step(m, step)
+
+        @pl.when(step == steps)
+        def _():
+            for sub in range(SUBS):
+                for way in range(2):
+                    cols = cols_of(way, sub)
+                    give[:, cols] = total(0, way, sub) - keep * bc_ref[:, cols]
+                    swap_copy(way, sub).start()
+
+        return carry
+
+    lax.fori_loop(0, 2 * steps, half_step, 0)
     for sub in range(SUBS):
         for way in range(2):
             cols = cols_of(way, sub)
@@ -573,7 +621,9 @@
 
     lax.fori_loop(0, steps, drain, 0)
     for m in range(2):
-        remote(acc.at[m, :, 1 - core], mate.at[m], mt_send.at[m], mt_recv.at[m, 0], buddy).wait_send()
+        for way in range(2):
+            for k in range(4):
+                mate_copy(m, way, k).wait_send()
     mask_copy().wait_send()
     open_copy().wait_send()
     for side in range(2):
@@ -626,10 +676,10 @@
             pltpu.VMEM((2, 2, SUBS, steps, rows, piece), F32),
             pltpu.VMEM((3, 2, d, 2 * quarter), BF16),
             pltpu.VMEM((4, 4 * quarter, ff // 2), BF16),
-            pltpu.VMEM((quarter, d), F32),
-            pltpu.VMEM((quarter, d), F32),
-            pltpu.VMEM((quarter, d), F32),
-            pltpu.VMEM((quarter, d), F32),
+            pltpu.VMEM((2 * quarter, d), F32),
+            pltpu.VMEM((2 * quarter, d), F32),
+            pltpu.VMEM((2 * quarter, d), F32),
+            pltpu.VMEM((2 * quarter, d), F32),
             pltpu.VMEM((quarter, ff), F32),
             pltpu.VMEM((quarter, ff), F32),
             pltpu.VMEM((eighth, ff), F32),
@@ -654,8 +704,8 @@
             dma((2,)),
             dma((2, 2, SUBS, steps)),
             dma((2, 2, SUBS, steps)),
-            dma((2,)),
-            dma((2, nc)),
+            dma((2, 2, 4)),
+            dma((2, 2, 4)),
         ],
         compiler_params=pltpu.CompilerParams(collective_id=0, has_side_effects=True, vmem_limit_bytes=66_500_000),
         cost_estimate=pl.CostEstimate(flops=32 * tokens * d * ff, bytes_accessed=100 * 2**20, transcendentals=0),

time: 203 us -> 185 us (0.911); the launches traced: 200 us -> 184 us
  Pallas kernels: 193 us -> 178 us
    pallas_call x1, Pallas kernels: 193 us -> 178 us  [body(): pl.pallas_call(functools.partial(kernel, n), out_shape=[shape(tokens, ff)...]
where the time goes in v1:
time: 185 us; the launch traced here: 184 us
  Pallas kernels  178 us (96%)
  local copies, waits for them, and re-layouts  5.55 us (3%)
    pallas_call x1, Pallas kernels, body(): pl.pallas_call(functools.partial(kernel, n), out_shape=[shape(tokens, ff)...  178 us
    unnamed x4, local copies, waits for them, and re-layouts  5.55 us

profile of v1, /device:TPU:0, one launch (start us, length us, event | category | flops | bytes accessed | tf_op | source)
XLA Modules:
  0.0 183.8 jit_solution(838478229768677456)
XLA Ops:
  0.6 177.6 %shard_map.104 = (f32[512,2048]{1,0:T(8,128)}, f32[64,2048]{1,0:T(8,128)}, f32[2,8,2,64,2048]{4,3,2,1,0:T(8,128)}, f32[512,1024]{1,0:T(8,128)}, f32[512,1024]{1,...) custom-call(f32[512,1024]{1,0:T(8,128)} %bitcast.16, f32[512,2048]{1,0:T(8,128)} %bitcast.13, ...), custom_call_target="tpu_custom_call" | custom-call | flops 34359738368 | bytes 104857600 | tf_op jit(solution)/shard_map/pallas_call | solution.py:659
  178.3 0.0 copy-start
  178.3 4.8 %copy.13 = f32[1,512,2048]{2,1,0:T(8,128)} copy(f32[1,512,2048]{2,1,0:T(8,128)} %bitcast.11) | data formatting | bytes 8388608
  183.0 0.0 copy-done
  183.0 0.8 copy.14
Async XLA Ops:
  178.3 4.8 %copy-start = (f32[64,2048]{1,0:T(8,128)S(1)}, f32[64,2048]{1,0:T(8,128)}, u32[]{:S(2)}) copy-start(f32[64,2048]{1,0:T(8,128)} %get-tuple-element.5) | copy-start | bytes 1572868

commit v2 on v1

--- a/solution.py
+++ b/solution.py
@@ -50,7 +50,7 @@
     w_ref,
     fb_ref,
     bc_ref,
-    y_ref,
+    ybuf,
     dw_ref,
     wts,
     rx,
@@ -71,7 +71,6 @@
     sb,
     sg2,
     tiles,
-    ybuf,
     own_w,
     got_w,
     delta,
@@ -79,7 +78,6 @@
     got,
     ld_sem,
     tile_sem,
-    y_sem,
     lc_sem,
     xs_send,
     xs_recv,
@@ -120,7 +118,9 @@
             src_ref=src, dst_ref=dst, send_sem=send, recv_sem=recv, device_id=device, device_id_type=MESH
         )
 
-    own_w[...] = w_ref[...] - fb_ref[...]
+    masks = [pltpu.make_async_copy(w_ref, own_w, ld_sem.at[0]), pltpu.make_async_copy(fb_ref, delta, ld_sem.at[1])]
+    for copy in masks:
+        copy.start()
     barrier = pltpu.get_barrier_semaphore()
     for device in (other, buddy, ahead, behind):
         pl.semaphore_signal(barrier, inc=1, device_id=device, device_id_type=MESH)
@@ -334,6 +334,9 @@
         lax.fori_loop(tile_from, tile_to, tile, 0)
 
     begin_gather(0, fb_ref)
+    for copy in masks:
+        copy.wait()
+    own_w[...] = own_w[...] - delta[...]
     mask_copy().start()
     for side in range(2):
 
@@ -516,7 +519,6 @@
             fetch(m, t, buf).wait()
         weight = split(tiles[0, buf].reshape(d, TILE) + keep * tiles[1, buf].reshape(d, TILE))
         ybuf[:, cols] = ybuf[:, cols] + product((right[2], right[3]), weight)
-        pltpu.make_async_copy(ybuf.at[:, cols], y_ref.at[:, cols], y_sem.at[t]).start()
 
     second(0)
     sum_start(0)
@@ -530,6 +532,29 @@
             return carry
 
         lax.fori_loop(turn * nt // 3, (turn + 1) * nt // 3, one, 0)
+
+    def drain_gather(step, carry):
+        for m in range(2):
+            for way in range(2):
+                for sub in range(SUBS):
+                    gather_copy(m, way, sub, step).wait_send()
+        return carry
+
+    def drain_early():
+        lax.fori_loop(0, steps, drain_gather, 0)
+        for m in range(2):
+            for way in range(2):
+                for k in range(4):
+                    mate_copy(m, way, k).wait_send()
+        mask_copy().wait_send()
+        for side in range(2):
+
+            @pl.when(party == side)
+            def _():
+                for j in range(2):
+                    for copy in chunk_copies(side, j):
+                        copy.wait_send()
+        open_copy().wait_send()
 
     def forward(work):
         @pl.when(work == 3)
@@ -555,6 +580,13 @@
         def _():
             several(second_tile, work - late - 1)
 
+        @pl.when(work == late + 4)
+        def _():
+            drain_early()
+            triple = load(bc_ref, got_w, 0)
+            triple.start()
+            triple.wait()
+
         @pl.when(work == late)
         def _():
             for m in range(2):
@@ -595,7 +627,7 @@
             for sub in range(SUBS):
                 for way in range(2):
                     cols = cols_of(way, sub)
-                    give[:, cols] = total(0, way, sub) - keep * bc_ref[:, cols]
+                    give[:, cols] = total(0, way, sub) - keep * got_w[:, cols]
                     swap_copy(way, sub).start()
 
         return carry
@@ -604,7 +636,7 @@
     for sub in range(SUBS):
         for way in range(2):
             cols = cols_of(way, sub)
-            dw_ref[:, cols] = total(1, way, sub) + keep * bc_ref[:, cols]
+            dw_ref[:, cols] = total(1, way, sub) + keep * got_w[:, cols]
     for sub in range(SUBS):
         for way in range(2):
             cols = cols_of(way, sub)
@@ -615,31 +647,13 @@
         for m in range(2):
             for way in range(2):
                 for sub in range(SUBS):
-                    gather_copy(m, way, sub, step).wait_send()
                     sum_copy(m, way, sub, step, slots.at[m, way, sub, step]).wait_send()
         return carry
 
     lax.fori_loop(0, steps, drain, 0)
-    for m in range(2):
-        for way in range(2):
-            for k in range(4):
-                mate_copy(m, way, k).wait_send()
-    mask_copy().wait_send()
-    open_copy().wait_send()
-    for side in range(2):
-
-        @pl.when(party == side)
-        def _():
-            for j in range(2):
-                for copy in chunk_copies(side, j):
-                    copy.wait_send()
-
     for way in range(2):
         for sub in range(SUBS):
             swap_copy(way, sub).wait_send()
-    for t in range(nt):
-        cols = pl.ds(t * TILE, TILE)
-        pltpu.make_async_copy(ybuf.at[:, cols], y_ref.at[:, cols], y_sem.at[t]).wait()
 
 
 def body(n, x_share, w_share, g_share, fwd_a, fwd_b, fwd_c, bwd_a, bwd_b, bwd_c):
@@ -659,8 +673,8 @@
     outs = pl.pallas_call(
         functools.partial(kernel, n),
         out_shape=[
-            shape(tokens, ff),
-            shape(rows, ff),
+            pltpu.VMEM((tokens, ff), F32),
+            pltpu.VMEM((rows, ff), F32),
             shape(2, nc, 2, rows, ff),
             shape(tokens, d),
             shape(tokens, d),
@@ -668,8 +682,8 @@
             shape(tokens, d),
             shape(tokens, d),
         ],
-        in_specs=[hbm] * 6 + [vmem] * 3,
-        out_specs=[hbm, vmem] + [hbm] * 6,
+        in_specs=[hbm] * 9,
+        out_specs=[vmem, vmem] + [hbm] * 6,
         scratch_shapes=[
             pltpu.VMEM((2, nc, 2, rows, ff), F32),
             pltpu.VMEM((2, nc, rows, ff), F32),
@@ -684,7 +698,6 @@
             pltpu.VMEM((quarter, ff), F32),
             pltpu.VMEM((eighth, ff), F32),
             pltpu.VMEM((2, 2, nc, 2, rows, TILE), F32),
-            pltpu.VMEM((tokens, ff), F32),
             pltpu.VMEM((rows, ff), F32),
             pltpu.VMEM((rows, ff), F32),
             pltpu.VMEM((rows, ff), F32),
@@ -692,7 +705,6 @@
             pltpu.VMEM((rows, ff), F32),
             dma((7,)),
             dma((2, 2)),
-            dma((ff // TILE,)),
             dma((2,)),
             dma((6,)),
             dma((6,)),
@@ -707,7 +719,7 @@
             dma((2, 2, 4)),
             dma((2, 2, 4)),
         ],
-        compiler_params=pltpu.CompilerParams(collective_id=0, has_side_effects=True, vmem_limit_bytes=66_500_000),
+        compiler_params=pltpu.CompilerParams(collective_id=0, has_side_effects=True, vmem_limit_bytes=61_500_000),
         cost_estimate=pl.CostEstimate(flops=32 * tokens * d * ff, bytes_accessed=100 * 2**20, transcendentals=0),
     )(
         x_share[0],

time: 185 us -> 180 us (0.973)
  Pallas kernels: 178 us -> 175 us
  local copies, waits for them, and re-layouts: 5.55 us -> 2.81 us
    unnamed x4 -> x2, local copies, waits for them, and re-layouts: 5.55 us -> 2.81 us
    pallas_call x1, Pallas kernels: 178 us -> 175 us  [body(): pl.pallas_call(functools.partial(kernel, n), out_shape=[pltpu.VMEM((token...]
where the time goes in v2:
time: 180 us; the launch traced here: 179 us
  Pallas kernels  175 us (97%)
  local copies, waits for them, and re-layouts  2.81 us (2%)
    pallas_call x1, Pallas kernels, body(): pl.pallas_call(functools.partial(kernel, n), out_shape=[pltpu.VMEM((token...  175 us

profile of v2, /device:TPU:0, one launch (start us, length us, event | category | flops | bytes accessed | tf_op | source)
XLA Modules:
  0.0 178.8 jit_solution(12687445950188948531)
XLA Ops:
  0.6 175.4 %shard_map.104 = (f32[512,2048]{1,0:T(8,128)S(1)}, f32[64,2048]{1,0:T(8,128)S(1)}, f32[2,8,2,64,2048]{4,3,2,1,0:T(8,128)}, f32[512,1024]{1,0:T(8,128)}, f32[512,...) custom-call(f32[512,1024]{1,0:T(8,128)} %bitcast.16, f32[512,2048]{1,0:T(8,128)} %bitcast.13, ...), custom_call_target="tpu_custom_call" | custom-call | flops 34359738368 | bytes 104857600 | tf_op jit(solution)/shard_map/pallas_call | solution.py:673
  176.0 2.0 %copy.13 = f32[1,512,2048]{2,1,0:T(8,128)} copy(f32[1,512,2048]{2,1,0:T(8,128)S(1)} %bitcast.11) | data formatting | bytes 8388608
  178.0 0.8 copy.14

commit v3 on v2

--- a/solution.py
+++ b/solution.py
@@ -70,6 +70,9 @@
     sg,
     sb,
     sg2,
+    vx,
+    va,
+    vg,
     tiles,
     own_w,
     got_w,
@@ -132,14 +135,18 @@
         if side == 0:
             everything = pl.ds(start, 2 * quarter)
             tail = pl.ds(start + 3 * eighth, eighth)
+            to_x = rx.at[everything] if j == 0 else vx
+            to_g = rg if j == 0 else vg
             return [
-                remote(x_ref.at[everything], rx.at[everything], xs_send.at[k], xs_recv.at[k], other),
-                remote(g_ref.at[tail], rg.at[pl.ds(j * eighth, eighth)], xs_send.at[k + 1], xs_recv.at[k + 1], other),
+                remote(x_ref.at[everything], to_x, xs_send.at[k], xs_recv.at[k], other),
+                remote(g_ref.at[tail], to_g, xs_send.at[k + 1], xs_recv.at[k + 1], other),
             ]
         head = pl.ds(start, 3 * eighth)
+        local = pl.ds(0, 3 * eighth)
+        to_x, to_a = (rx.at[head], ra.at[head]) if j == 0 else (vx.at[local], va.at[local])
         return [
-            remote(x_ref.at[head], rx.at[head], xs_send.at[k], xs_recv.at[k], other),
-            remote(ba_ref.at[head], ra.at[head], xs_send.at[k + 1], xs_recv.at[k + 1], other),
+            remote(x_ref.at[head], to_x, xs_send.at[k], xs_recv.at[k], other),
+            remote(ba_ref.at[head], to_a, xs_send.at[k + 1], xs_recv.at[k + 1], other),
         ]
 
     def mask_copy():
@@ -264,37 +271,36 @@
         start = 2 * j * quarter
         whole = slice(0, 2 * quarter)
         many = 3 * eighth
+        in_x, in_a, in_g = (sx2, sa2, sg2) if j == 0 else (vx, va, vg)
+
+        def fetch_all(copies):
+            if j == 0:
+                for copy in copies:
+                    copy.start()
+                for copy in copies:
+                    copy.wait()
 
         @pl.when(first)
         def _():
             for copy in chunk_copies(1, j):
                 copy.wait_recv()
-            some = pl.ds(start, many)
-            more = [load(rx.at[some], sx2.at[pl.ds(0, many)], 4), load(ra.at[some], sa2.at[pl.ds(0, many)], 5)]
-            for copy in more:
-                copy.start()
-            for copy in more:
-                copy.wait()
-            sx2[many:, :] = jnp.zeros((eighth, d), F32)
-            sa2[many:, :] = jnp.zeros((eighth, d), F32)
+            if j == 0:
+                some, local = pl.ds(start, many), pl.ds(0, many)
+                fetch_all([load(rx.at[some], sx2.at[local], 4), load(ra.at[some], sa2.at[local], 5)])
+            in_x[many:, :] = jnp.zeros((eighth, d), F32)
+            in_a[many:, :] = jnp.zeros((eighth, d), F32)
             sx[many:, :] = jnp.zeros((eighth, d), F32)
-            put_left(0, whole, sa2[...])
-            put_left(1, whole, (sx[...] + sx2[...]) - sa2[...])
+            put_left(0, whole, in_a[...])
+            put_left(1, whole, (sx[...] + in_x[...]) - in_a[...])
 
         @pl.when(jnp.logical_not(first))
         def _():
             for copy in chunk_copies(0, j):
                 copy.wait_recv()
-            more = [
-                load(rx.at[pl.ds(start, 2 * quarter)], sx2, 4),
-                load(rg.at[pl.ds(j * eighth, eighth)], sg2, 5),
-            ]
-            for copy in more:
-                copy.start()
-            for copy in more:
-                copy.wait()
-            put_right(0, slice(many, 2 * quarter), sg[eighth:, :] + sg2[...])
-            sx[...] = sx[...] + sx2[...]
+            if j == 0:
+                fetch_all([load(rx.at[pl.ds(start, 2 * quarter)], sx2, 4), load(rg, sg2, 5)])
+            put_right(0, slice(many, 2 * quarter), sg[eighth:, :] + in_g[...])
+            sx[...] = sx[...] + in_x[...]
             put_left(0, whole, sx[...] - sa[...])
             put_left(2, whole, sx[...])
 
@@ -303,7 +309,7 @@
     group = d // 4
     per = group // (2 * rows)
 
-    def gradient_rows(j, q, tile_from, tile_to):
+    def gradient_rows(j, q, tile_from, tile_to, only=None):
         at = pl.ds(pl.multiple_of(q * group, group), group)
         chips = pl.ds(q * per, per)
 
@@ -321,14 +327,12 @@
 
             shared = multiply(2, 1)
             shape = (per, 2, rows, WIDE)
-            foreign = (multiply(0, 0) + keep * shared).reshape(shape)
-            mine = (multiply(1, 0) + sign * shared).reshape(shape)
-            if j == 0:
-                acc[0, chips, :, :, cols] = foreign
-                acc[1, chips, :, :, cols] = mine
-            else:
-                acc[0, chips, :, :, cols] = acc[0, chips, :, :, cols] + foreign
-                acc[1, chips, :, :, cols] = acc[1, chips, :, :, cols] + mine
+            for m in range(2):
+                if only is None or only == m:
+                    value = (multiply(m, 0) + (sign if m else keep) * shared).reshape(shape)
+                    if j == 1:
+                        value = acc[m, chips, :, :, cols] + value
+                    acc[m, chips, :, :, cols] = value
             return carry
 
         lax.fori_loop(tile_from, tile_to, tile, 0)
@@ -388,11 +392,14 @@
             def _():
                 gradient_rows(0, 2 * (i - early - 1) + 1, 0, ff // WIDE)
 
+        @pl.when(i == early + 2)
+        def _():
+            owned(1)
+
         return carry
 
     lax.fori_loop(0, steps + LAG - 1, gather_step, 0)
 
-    owned(1)
     received(1)
     zs, span = nc // 2, nc // 8
 
@@ -444,9 +451,9 @@
             mate_copy(m, way, step).wait_recv()
 
     def sum_start(m):
-        mate_arrivals(m, 0)
-        for sub in range(SUBS):
-            for way in range(2):
+        for way in range(2):
+            mate_copy(m, way, 0).wait_recv()
+            for sub in range(SUBS):
                 owner, cols = owner_of(way, 0), cols_of(way, sub)
                 acc[m, owner, core, :, cols] = acc[m, owner, core, :, cols] + mate[m, owner, :, cols]
                 sum_copy(m, way, sub, 0, acc.at[m, owner, core, :, cols]).start()
@@ -520,8 +527,16 @@
         weight = split(tiles[0, buf].reshape(d, TILE) + keep * tiles[1, buf].reshape(d, TILE))
         ybuf[:, cols] = ybuf[:, cols] + product((right[2], right[3]), weight)
 
-    second(0)
-    sum_start(0)
+    for m in range(2):
+
+        def opening(way, carry):
+            gradient_rows(1, group_at(way, 0), way * (ff // 2 // WIDE), (way + 1) * (ff // 2 // WIDE), m)
+            mate_copy(m, way, 0).start()
+            return carry
+
+        lax.fori_loop(0, 2, opening, 0)
+        if m == 0:
+            sum_start(0)
     second(1)
     pass_on(1, steps - 1)
     late = 2 * steps - 6
@@ -676,9 +691,9 @@
             pltpu.VMEM((tokens, ff), F32),
             pltpu.VMEM((rows, ff), F32),
             shape(2, nc, 2, rows, ff),
-            shape(tokens, d),
-            shape(tokens, d),
-            shape(tokens // 4, ff),
+            shape(tokens // 2, d),
+            shape(tokens // 2, d),
+            shape(tokens // 8, ff),
             shape(tokens, d),
             shape(tokens, d),
         ],
@@ -696,6 +711,9 @@
             pltpu.VMEM((2 * quarter, d), F32),
             pltpu.VMEM((quarter, ff), F32),
             pltpu.VMEM((quarter, ff), F32),
+            pltpu.VMEM((eighth, ff), F32),
+            pltpu.VMEM((2 * quarter, d), F32),
+            pltpu.VMEM((2 * quarter, d), F32),
             pltpu.VMEM((eighth, ff), F32),
             pltpu.VMEM((2, 2, nc, 2, rows, TILE), F32),
             pltpu.VMEM((rows, ff), F32),

time: 180 us -> 178 us (0.989)
  no operation moved by 1% of the time
where the time goes in v3:
time: 178 us; the launch traced here: 177 us
  Pallas kernels  174 us (98%)
  local copies, waits for them, and re-layouts  2.81 us (2%)
    pallas_call x1, Pallas kernels, body(): pl.pallas_call(functools.partial(kernel, n), out_shape=[pltpu.VMEM((token...  174 us

profile of v3, /device:TPU:0, one launch (start us, length us, event | category | flops | bytes accessed | tf_op | source)
XLA Modules:
  0.0 177.2 jit_solution(573901436375944522)
XLA Ops:
  0.6 173.7 %shard_map.104 = (f32[512,2048]{1,0:T(8,128)S(1)}, f32[64,2048]{1,0:T(8,128)S(1)}, f32[2,8,2,64,2048]{4,3,2,1,0:T(8,128)}, f32[256,1024]{1,0:T(8,128)}, f32[256,...) custom-call(f32[512,1024]{1,0:T(8,128)} %bitcast.16, f32[512,2048]{1,0:T(8,128)} %bitcast.13, ...), custom_call_target="tpu_custom_call" | custom-call | flops 34359738368 | bytes 104857600 | tf_op jit(solution)/shard_map/pallas_call | solution.py:688
  174.3 2.0 %copy.13 = f32[1,512,2048]{2,1,0:T(8,128)} copy(f32[1,512,2048]{2,1,0:T(8,128)S(1)} %bitcast.11) | data formatting | bytes 8388608
  176.4 0.8 copy.14

commit v4 on v3

--- a/solution.py
+++ b/solution.py
@@ -539,7 +539,7 @@
             sum_start(0)
     second(1)
     pass_on(1, steps - 1)
-    late = 2 * steps - 6
+    late = 2 * steps - 5
 
     def several(tile, turn):
         def one(t, carry):
@@ -595,7 +595,7 @@
         def _():
             several(second_tile, work - late - 1)
 
-        @pl.when(work == late + 4)
+        @pl.when(work == late + 3)
         def _():
             drain_early()
             triple = load(bc_ref, got_w, 0)

time: 178 us -> 178 us (level)
  no operation moved by 1% of the time
where the time goes in v4:
time: 178 us; the launch traced here: 177 us
  Pallas kernels  174 us (98%)
  local copies, waits for them, and re-layouts  2.81 us (2%)
    pallas_call x1, Pallas kernels, body(): pl.pallas_call(functools.partial(kernel, n), out_shape=[pltpu.VMEM((token...  174 us

profile of v4, /device:TPU:0, one launch (start us, length us, event | category | flops | bytes accessed | tf_op | source)
XLA Modules:
  0.0 177.2 jit_solution(7465451334347406935)
XLA Ops:
  0.6 173.7 %shard_map.104 = (f32[512,2048]{1,0:T(8,128)S(1)}, f32[64,2048]{1,0:T(8,128)S(1)}, f32[2,8,2,64,2048]{4,3,2,1,0:T(8,128)}, f32[256,1024]{1,0:T(8,128)}, f32[256,...) custom-call(f32[512,1024]{1,0:T(8,128)} %bitcast.16, f32[512,2048]{1,0:T(8,128)} %bitcast.13, ...), custom_call_target="tpu_custom_call" | custom-call | flops 34359738368 | bytes 104857600 | tf_op jit(solution)/shard_map/pallas_call | solution.py:688
  174.3 2.0 %copy.13 = f32[1,512,2048]{2,1,0:T(8,128)} copy(f32[1,512,2048]{2,1,0:T(8,128)S(1)} %bitcast.11) | data formatting | bytes 8388608
  176.4 0.8 copy.14
